TPU v7x, 256 devices: a whole 4x4x8 slice. The times are simulated.
256 devices in a mesh: seq: 32 (over x, z), tp: 4 (over y), lat: 2 (over core).
Axes of the slice: x: 4, y: 4, z: 8, core: 2. Of those that a mesh axis runs over, the one named last changes fastest.
Arguments:
- tokens: bfloat16 [24576, 8192], P(('seq', 'lat'), 'tp'), may hold values from -6 to 6
- active: int32 [24576, 4], P(('seq', 'lat')), may hold values from 0 to 255, all different within a row; in each aligned block of 384 rows (0 to 383, 384 to 767, ...) at most 9 rows name the same one
- placement_map: int32 [256], replicated, may hold values from 0 to 255, each once
- enc_weight: bfloat16 [8192, 32768], P('tp', ('seq', 'lat')), may hold values from -0.0625 to 0.0625
- enc_bias: float32 [32768], P(('seq', 'lat')), may hold values from -3 to 3
- dec_weight: bfloat16 [32768, 8192], P(('seq', 'lat'), 'tp'), may hold values from -0.375 to 0.375
- dec_bias: float32 [8192], P('tp'), may hold values from -3 to 3
Outputs:
- recon: bfloat16 [24576, 8192], P(('seq', 'lat'), 'tp')
Inputs may be any that keep to these rules, and one draw needn't show every extreme that they name: `active`: the 4 blocks of one token are different. Among the rows of one device (aligned blocks of 384 rows) no block is named more than 9 times, and some block is named exactly 9 times. `placement_map`: each column block appears once.
All inputs are finite; a program needn't handle non-finite values.
Results may differ from a plain program's by a relative error of at most 0.0061.
Values may be sent and summed in bfloat16 or wider, within the bound.
A program may use at most 128 MiB of HBM per device.

v0:
```python
import jax
import jax.numpy as jnp
from jax import lax
from jax.sharding import PartitionSpec as P


def local(tokens, active, placement_map, enc_weight, enc_bias, dec_weight, dec_bias):
    rows, width = tokens.shape
    top = active.shape[1]
    nblocks = placement_map.shape[0]
    seq_count = lax.axis_size("seq")
    lat_count = lax.axis_size("lat")
    owners = seq_count * lat_count
    local_blocks = nblocks // owners
    block_width = enc_bias.shape[0] // local_blocks
    capacity = 3 * rows * top // (2 * nblocks)
    centered = (tokens.astype(jnp.float32) - dec_bias[None, :]).astype(jnp.bfloat16)
    block_ids = jnp.arange(nblocks, dtype=jnp.int32)
    matches = (active[:, :, None] == block_ids[None, None, :]).astype(jnp.int32)
    position = jnp.sum(matches * placement_map[None, None, :], axis=2).reshape(-1)
    pos_hot = (position[:, None] == block_ids[None, :]).astype(jnp.int32)
    rank = jnp.sum((jnp.cumsum(pos_hot, axis=0) - 1) * pos_hot, axis=1)
    target = position * capacity + rank
    pair_row = jnp.arange(rows * top, dtype=jnp.int32) // top
    slot_row = jnp.zeros((nblocks * capacity,), jnp.int32).at[target].set(pair_row)
    filled = jnp.zeros((nblocks * capacity,), jnp.bool_).at[target].set(True)
    outgoing = jnp.where(filled[:, None], centered[slot_row], jnp.zeros((), jnp.bfloat16))
    outgoing = outgoing.reshape(owners, local_blocks, capacity, width)
    enc_blocks = enc_weight.reshape(width, local_blocks, block_width)
    bias_blocks = enc_bias.reshape(local_blocks, block_width)
    dec_blocks = dec_weight.reshape(local_blocks, block_width, width)
    preact = jnp.einsum(
        "sbcd,dbh->sbch",
        lax.all_to_all(outgoing, ("seq", "lat"), split_axis=0, concat_axis=0, tiled=True),
        enc_blocks,
        preferred_element_type=jnp.float32,
    )
    summed = lax.psum(preact, "tp")
    codes = jnp.maximum(summed + bias_blocks[None, :, None, :], 0.0).astype(jnp.bfloat16)
    returned = lax.all_to_all(
        jnp.einsum("sbch,bhd->sbcd", codes, dec_blocks, preferred_element_type=jnp.float32).astype(
            jnp.bfloat16
        ),
        ("seq", "lat"),
        split_axis=0,
        concat_axis=0,
        tiled=True,
    )
    returned = returned.reshape(nblocks * capacity, width)
    contrib = returned[target].reshape(rows, top, width).astype(jnp.float32)
    return (jnp.sum(contrib, axis=1) + dec_bias[None, :]).astype(jnp.bfloat16)


def solution(mesh):
    return jax.shard_map(
        local,
        mesh=mesh,
        in_specs=(
            P(("seq", "lat"), "tp"),
            P(("seq", "lat"), None),
            P(),
            P("tp", ("seq", "lat")),
            P(("seq", "lat")),
            P(("seq", "lat"), "tp"),
            P("tp"),
        ),
        out_specs=P(("seq", "lat"), "tp"),
        check_vma=False,
    )
```

profile of v0, /device:TPU:1, one launch (start us, length us, event | category | flops | bytes accessed | tf_op | source)
XLA Modules:
  0.0 689.2 jit_solution(1939051492768150350)
XLA Ops:
  6.5 0.0 copy-start
  6.5 1.4 select_reduce_fusion
  7.9 0.1 copy.29
  8.0 0.1 eq.45
  8.2 0.1 eq.41
  8.4 0.1 copy.31
  8.5 0.3 fusion.3
  8.8 0.0 copy-start.2
  8.8 1.3 copy-done.2
  10.2 1.8 add_add_fusion
  12.0 0.0 copy-start.3
  12.1 2.1 copy.32
  14.1 0.1 copy.28
  14.3 0.2 mul.31
  14.4 1.9 fusion.5
  16.4 6.4 scatter_custom_fusion.1
  22.8 0.0 copy-done.3
  22.8 2.9 subtract_convert_fusion
  25.7 20.0 %gather_fusion = bf16[2304,2048]{1,0:T(8,128)(2,1)} fusion(bf16[384,2048]{1,0:T(8,128)(2,1)} %subtract_convert_fusion, s32[3072]{0:T(1024)S(1)} %pad_clamp_fusion), kind=kCustom, calls=%fused_computation | custom fusion | bytes 18883584 | tf_op jit(solution)/shard_map/gather | solution.py:27
  45.7 15.1 %gather.9 = bf16[64,4,9,2048]{3,2,1,0:T(8,128)(2,1)} reshape(bf16[2304,2048]{1,0:T(8,128)(2,1)} %gather_fusion) | data formatting | bytes 18874368 | tf_op jit(solution)/shard_map/gather | solution.py:27
  60.8 11.2 %scatter_custom_fusion = pred[2304]{0:T(1024)(128)(4,1)S(1)} fusion(s32[1536]{0:T(1024)S(1)} %fusion.17, pred[1536]{0:T(1024)(128)(4,1)S(1)} %broadcast.82, pred[]{:T(512)} %constant.16.clone.1), kind=kCustom, calls=%fused_computation.40 | custom fusion | bytes 2305 | tf_op jit(solution)/shard_map/scatter | solution.py:26
  72.0 0.2 broadcast_in_dim.35
  72.2 8.3 %broadcast_select_fusion = bf16[64,4,9,2048]{3,2,1,0:T(8,128)(2,1)S(1)} fusion(bf16[64,4,9,2048]{3,2,1,0:T(8,128)(2,1)} %gather.9, pred[64,4,9]{2,1,0:T(4,128)(4,1)S(1)} %broadcast_in_dim.35), kind=kLoop, calls=%fused_computation.4 | loop fusion | flops 4718592 | bytes 18876672 | tf_op jit(solution)/shard_map/jit(_where)/select_n | solution.py:27
  80.5 19.6 %copy.33 = bf16[64,4,9,2048]{3,1,2,0:T(4,128)(2,1)} copy(bf16[64,4,9,2048]{3,2,1,0:T(8,128)(2,1)S(1)} %broadcast_select_fusion) | data formatting | bytes 18874368 | tf_op jit(solution)/shard_map/jit(_where)/select_n | solution.py:27
  100.1 13.2 %all-to-all-start = ((bf16[64,4,9,2048]{3,1,2,0:T(4,128)(2,1)}), bf16[64,4,9,2048]{3,1,2,0:T(4,128)(2,1)}, u32[]{:S(2)}, u32[]{:S(2)}) async-start(bf16[64,4,9,2048]{3,1,2,0:T(4,128)(2,1)} %copy.33), calls=%async_computation | async-start | bytes 18874368 | tf_op jit(solution)/shard_map/all_to_all | solution.py:34
  113.2 0.3 all-reduce.2.cloned.1.call-start
  113.5 4.0 reshape.73
  117.5 204.0 %all-to-all-done = bf16[64,4,9,2048]{3,1,2,0:T(4,128)(2,1)} async-done(((bf16[64,4,9,2048]{3,1,2,0:T(4,128)(2,1)}), bf16[64,4,9,2048]{3,1,2,0:T(4,128)(2,1)}, u32[]{:S(2)}, u32[]{:S(2)}) %all-to-all-start) | async-done | bytes 9437216 | tf_op jit(solution)/shard_map/all_to_all | solution.py:34
  321.5 0.0 copy-start.4
  321.5 10.5 %fusion.6 = f32[64,4,9,128]{3,0,2,1:T(8,128)} fusion(bf16[2048,4,128,1]{2,1,0,3:T(4,128)(2,1)} %bitcast.22, bf16[64,4,9,2048]{3,1,2,0:T(4,128)(2,1)} %all-to-all-done), kind=kOutput, calls=%fused_computation.20 | convolution fusion | flops 1207959552 | bytes 12713984 | tf_op jit(solution)/shard_map/sbcd,dbh->sbch/dot_general | solution.py:32
  332.0 0.0 all-reduce.2.cloned.1.call-update
  332.0 47.5 %all-reduce.2.cloned.1.call-done = f32[64,4,9,128]{3,0,2,1:T(8,128)} async-done(((f32[64,4,9,128]{3,0,2,1:T(8,128)}), f32[64,4,9,128]{3,0,2,1:T(8,128)}) %all-reduce.2.cloned.1.call-update) | async-done | bytes 1179664 | tf_op jit(solution)/shard_map/psum | solution.py:38
  379.5 0.0 copy-done
  379.5 0.0 copy-done.4
  379.5 4.1 convert_bitcast_fusion
  383.6 7.3 %copy.36 = bf16[64,4,9,2048]{3,1,2,0:T(4,128)(2,1)} copy(bf16[64,4,9,2048]{3,0,2,1:T(8,128)(2,1)S(1)} %convert_bitcast_fusion) | data formatting | bytes 18874368 | tf_op jit(solution)/shard_map/convert_element_type | solution.py:41
  390.9 11.9 %all-to-all-start.1 = ((bf16[64,4,9,2048]{3,1,2,0:T(4,128)(2,1)}), bf16[64,4,9,2048]{3,1,2,0:T(4,128)(2,1)}, u32[]{:S(2)}, u32[]{:S(2)}) async-start(bf16[64,4,9,2048]{3,1,2,0:T(4,128)(2,1)} %copy.36), calls=%async_computation.1 | async-start | bytes 18874368 | tf_op jit(solution)/shard_map/all_to_all | solution.py:40
  402.9 208.2 %all-to-all-done.1 = bf16[64,4,9,2048]{3,1,2,0:T(4,128)(2,1)} async-done(((bf16[64,4,9,2048]{3,1,2,0:T(4,128)(2,1)}), bf16[64,4,9,2048]{3,1,2,0:T(4,128)(2,1)}, u32[]{:S(2)}, u32[]{:S(2)}) %all-to-all-start.1) | async-done | bytes 9437216 | tf_op jit(solution)/shard_map/all_to_all | solution.py:40
  611.1 10.7 %copy.37 = bf16[64,4,9,2048]{3,2,1,0:T(8,128)(2,1)} copy(bf16[64,4,9,2048]{3,1,2,0:T(4,128)(2,1)} %all-to-all-done.1) | data formatting | bytes 18874368 | tf_op jit(solution)/shard_map/all_to_all | solution.py:40
  621.8 15.8 %reshape.75 = bf16[2304,2048]{1,0:T(8,128)(2,1)} reshape(bf16[64,4,9,2048]{3,2,1,0:T(8,128)(2,1)} %copy.37) | data formatting | bytes 18874368 | tf_op jit(solution)/shard_map/reshape | solution.py:49
  637.6 17.6 %gather_fusion.1 = bf16[1536,2048]{1,0:T(8,128)(2,1)} fusion(bf16[2304,2048]{1,0:T(8,128)(2,1)} %reshape.75, s32[2048]{0:T(1024)S(1)} %pad_clamp_fusion.1), kind=kCustom, calls=%fused_computation.1 | custom fusion | bytes 12589056 | tf_op jit(solution)/shard_map/gather | solution.py:50
  655.2 11.9 %reshape.76 = f32[384,4,2048]{2,1,0:T(4,128)} reshape(bf16[1536,2048]{1,0:T(8,128)(2,1)} %gather_fusion.1) | data formatting | bytes 18874368 | tf_op jit(solution)/shard_map/convert_element_type | solution.py:50
  667.1 0.0 copy-start.1
  667.1 11.9 %reduce_sum.32 = f32[384,2048]{1,0:T(8,128)} reduce(f32[384,4,2048]{2,1,0:T(4,128)} %reshape.76, f32[]{:T(128)} %constant.42.clone.1), dimensions={1}, to_apply=%region_7.8 | reduce | flops 2359296 | bytes 15728644 | tf_op jit(solution)/shard_map/reduce_sum | solution.py:51
  679.0 3.4 add_convert_fusion
  682.4 0.0 copy-done.1
  (9 shorter events, 0.1 us)
Async XLA Ops:
  6.5 373.0 %copy-start = (bf16[512,2048]{1,0:T(8,128)(2,1)S(1)}, bf16[512,2048]{1,0:T(8,128)(2,1)}, u32[]{:S(2)}) copy-start(bf16[512,2048]{1,0:T(8,128)(2,1)} %param.12) | copy-start | bytes 6291460
  8.8 1.4 copy-start.2
  12.0 10.7 %copy-start.3 = (f32[2048]{0:T(1024)S(1)}, f32[2048]{0:T(1024)}, u32[]{:S(2)}) copy-start(f32[2048]{0:T(1024)} %param.13) | copy-start | bytes 24580
  100.1 221.4 %all-to-all-start = ((bf16[64,4,9,2048]{3,1,2,0:T(4,128)(2,1)}), bf16[64,4,9,2048]{3,1,2,0:T(4,128)(2,1)}, u32[]{:S(2)}, u32[]{:S(2)}) async-start(bf16[64,4,9,2048]{3,1,2,0:T(4,128)(2,1)} %copy.33), calls=%async_computation | async-start | bytes 18874368 | tf_op jit(solution)/shard_map/all_to_all | solution.py:34
  113.2 266.3 %all-reduce.2.cloned.1.call-start = ((), (), s32[]{:S(2)}) async-start(), calls=%async_computation.2 | async-start | bytes 2359296 | tf_op jit(solution)/shard_map/psum | solution.py:38
  321.5 58.0 %copy-start.4 = (f32[512]{0:T(512)S(1)}, f32[512]{0:T(512)}, u32[]{:S(2)}) copy-start(f32[512]{0:T(512)} %param.11) | copy-start | bytes 6148
  390.9 220.2 %all-to-all-start.1 = ((bf16[64,4,9,2048]{3,1,2,0:T(4,128)(2,1)}), bf16[64,4,9,2048]{3,1,2,0:T(4,128)(2,1)}, u32[]{:S(2)}, u32[]{:S(2)}) async-start(bf16[64,4,9,2048]{3,1,2,0:T(4,128)(2,1)} %copy.36), calls=%async_computation.1 | async-start | bytes 18874368 | tf_op jit(solution)/shard_map/all_to_all | solution.py:40
  667.1 15.3 %copy-start.1 = (bf16[512,2048]{1,0:T(8,128)(2,1)S(1)}, bf16[512,2048]{1,0:T(8,128)(2,1)}, u32[]{:S(2)}) copy-start(bf16[512,2048]{1,0:T(8,128)(2,1)} %param.12) | copy-start | bytes 6291460
Sparse Core Ops, SparseCore 0:
  332.1 47.3 all-reduce.1
where the time goes:
time: 691 us; the launch traced here: 689 us
  waiting for transfers between devices  460 us (67%)
  local copies, waits for them, and re-layouts  144 us (21%)
  other arithmetic  32 us (5%)
  starting transfers between devices  25.3 us (4%)
  matrix products  14.6 us (2%)
  between operations  13.6 us (2%)
    all_to_all x1, waiting for transfers between devices, local(): lax.all_to_all(jnp.einsum('sbch,bhd->sbcd', codes, dec_blocks, preferred_...  208 us
    all_to_all x1, waiting for transfers between devices, local(): lax.all_to_all(outgoing, ('seq', 'lat'), split_axis=0, concat_axis=0, til...  204 us
    psum x1, waiting for transfers between devices, local(): summed = lax.psum(preact, 'tp')  47.5 us
    gather x2, local copies, waits for them, and re-layouts, local(): centered[slot_row]  35 us
    select_n x1, local copies, waits for them, and re-layouts, local(): jnp.where(filled[:, None], centered[slot_row], jnp.zeros((), jnp.bfloat16))  19.6 us
    gather x1, local copies, waits for them, and re-layouts, local(): contrib = returned[target].reshape(rows, top, width).astype(jnp.float32)  17.6 us
    reshape x1, local copies, waits for them, and re-layouts, local(): returned = returned.reshape(nblocks * capacity, width)  15.8 us
  transfers between devices with their start and end apart: 3, of which 3 were waited for; matrix products, arithmetic and copies ran while one was open for 1% of the time, Pallas kernels for 0%

commit v1 on v0

--- a/solution.py
+++ b/solution.py
@@ -35,7 +35,11 @@
         enc_blocks,
         preferred_element_type=jnp.float32,
     )
-    summed = lax.psum(preact, "tp")
+    n_dev = lax.axis_size("tp")
+    summed, far = (preact, 1)
+    while far < n_dev:
+        summed = summed + lax.ppermute(summed, "tp", [(i, i ^ far) for i in range(n_dev)])
+        far = 2 * far
     codes = jnp.maximum(summed + bias_blocks[None, :, None, :], 0.0).astype(jnp.bfloat16)
     returned = lax.all_to_all(
         jnp.einsum("sbch,bhd->sbcd", codes, dec_blocks, preferred_element_type=jnp.float32).astype(

time: 691 us -> 680 us (0.984)
  between operations: 13.6 us -> 0.19 us
    ppermute x0 -> x2, waiting for transfers between devices: none -> 52.3 us  [local(): lax.ppermute(summed, 'tp', [(i, i ^ far) for i in range(n_dev)])]
    psum x1 -> x0, waiting for transfers between devices: 47.5 us -> none  [local(): summed = lax.psum(preact, 'tp')]
  transfers between devices with their start and end apart: 3 -> 4, of which waited for: 3 -> 4; matrix products, arithmetic and copies ran while one was open for 1% -> 1% of each run, Pallas kernels for 0% -> 0%
where the time goes in v1:
time: 680 us; the launch traced here: 679 us
  waiting for transfers between devices  465 us (68%)
  local copies, waits for them, and re-layouts  144 us (21%)
  other arithmetic  32.2 us (5%)
  starting transfers between devices  24.1 us (4%)
  matrix products  13.4 us (2%)
    all_to_all x1, waiting for transfers between devices, local(): lax.all_to_all(jnp.einsum('sbch,bhd->sbcd', codes, dec_blocks, preferred_...  208 us
    all_to_all x1, waiting for transfers between devices, local(): lax.all_to_all(outgoing, ('seq', 'lat'), split_axis=0, concat_axis=0, til...  204 us
    ppermute x2, waiting for transfers between devices, local(): lax.ppermute(summed, 'tp', [(i, i ^ far) for i in range(n_dev)])  52.3 us
    gather x2, local copies, waits for them, and re-layouts, local(): centered[slot_row]  35 us
    select_n x1, local copies, waits for them, and re-layouts, local(): jnp.where(filled[:, None], centered[slot_row], jnp.zeros((), jnp.bfloat16))  19.6 us
    gather x1, local copies, waits for them, and re-layouts, local(): contrib = returned[target].reshape(rows, top, width).astype(jnp.float32)  17.6 us
    reshape x1, local copies, waits for them, and re-layouts, local(): returned = returned.reshape(nblocks * capacity, width)  15.8 us
  transfers between devices with their start and end apart: 4, of which 4 were waited for; matrix products, arithmetic and copies ran while one was open for 1% of the time, Pallas kernels for 0%

profile of v1, /device:TPU:1, one launch (start us, length us, event | category | flops | bytes accessed | tf_op | source)
XLA Modules:
  0.0 678.6 jit_solution(11748574870754439867)
XLA Ops:
  0.0 0.0 copy-start
  0.0 1.4 select_reduce_fusion
  1.4 0.1 copy.32
  1.5 0.1 eq.45
  1.7 0.1 eq.41
  1.8 0.1 copy.34
  1.9 0.3 fusion.3
  2.3 0.0 copy-start.2
  2.3 1.3 copy-done.2
  3.7 1.8 add_add_fusion
  5.5 0.0 copy-start.3
  5.5 2.1 copy.35
  7.6 0.1 copy.31
  7.7 0.2 mul.31
  7.9 1.9 fusion.5
  9.8 6.4 scatter_custom_fusion.1
  16.2 0.0 copy-done.3
  16.2 2.9 subtract_convert_fusion
  19.2 20.0 %gather_fusion = bf16[2304,2048]{1,0:T(8,128)(2,1)} fusion(bf16[384,2048]{1,0:T(8,128)(2,1)} %subtract_convert_fusion, s32[3072]{0:T(1024)S(1)} %pad_clamp_fusion), kind=kCustom, calls=%fused_computation | custom fusion | bytes 18883584 | tf_op jit(solution)/shard_map/gather | solution.py:27
  39.2 15.1 %gather.9 = bf16[64,4,9,2048]{3,2,1,0:T(8,128)(2,1)} reshape(bf16[2304,2048]{1,0:T(8,128)(2,1)} %gather_fusion) | data formatting | bytes 18874368 | tf_op jit(solution)/shard_map/gather | solution.py:27
  54.2 11.2 %scatter_custom_fusion = pred[2304]{0:T(1024)(128)(4,1)S(1)} fusion(s32[1536]{0:T(1024)S(1)} %fusion.17, pred[1536]{0:T(1024)(128)(4,1)S(1)} %broadcast.82, pred[]{:T(512)} %constant.16.clone.1), kind=kCustom, calls=%fused_computation.40 | custom fusion | bytes 2305 | tf_op jit(solution)/shard_map/scatter | solution.py:26
  65.4 0.2 broadcast_in_dim.35
  65.7 8.3 %broadcast_select_fusion = bf16[64,4,9,2048]{3,2,1,0:T(8,128)(2,1)S(1)} fusion(bf16[64,4,9,2048]{3,2,1,0:T(8,128)(2,1)} %gather.9, pred[64,4,9]{2,1,0:T(4,128)(4,1)S(1)} %broadcast_in_dim.35), kind=kLoop, calls=%fused_computation.4 | loop fusion | flops 4718592 | bytes 18876672 | tf_op jit(solution)/shard_map/jit(_where)/select_n | solution.py:27
  74.0 19.6 %copy.36 = bf16[64,4,9,2048]{3,1,2,0:T(4,128)(2,1)} copy(bf16[64,4,9,2048]{3,2,1,0:T(8,128)(2,1)S(1)} %broadcast_select_fusion) | data formatting | bytes 18874368 | tf_op jit(solution)/shard_map/jit(_where)/select_n | solution.py:27
  93.5 13.2 %all-to-all-start = ((bf16[64,4,9,2048]{3,1,2,0:T(4,128)(2,1)}), bf16[64,4,9,2048]{3,1,2,0:T(4,128)(2,1)}, u32[]{:S(2)}, u32[]{:S(2)}) async-start(bf16[64,4,9,2048]{3,1,2,0:T(4,128)(2,1)} %copy.36), calls=%async_computation | async-start | bytes 18874368 | tf_op jit(solution)/shard_map/all_to_all | solution.py:34
  106.7 4.0 reshape.73
  110.7 204.3 %all-to-all-done = bf16[64,4,9,2048]{3,1,2,0:T(4,128)(2,1)} async-done(((bf16[64,4,9,2048]{3,1,2,0:T(4,128)(2,1)}), bf16[64,4,9,2048]{3,1,2,0:T(4,128)(2,1)}, u32[]{:S(2)}, u32[]{:S(2)}) %all-to-all-start) | async-done | bytes 9437216 | tf_op jit(solution)/shard_map/all_to_all | solution.py:34
  315.0 10.6 %fusion.6 = f32[64,4,9,128]{3,0,2,1:T(8,128)S(1)} fusion(bf16[2048,4,128,1]{2,1,0,3:T(4,128)(2,1)} %bitcast.22, bf16[64,4,9,2048]{3,1,2,0:T(4,128)(2,1)} %all-to-all-done), kind=kOutput, calls=%fused_computation.20 | convolution fusion | flops 1207959552 | bytes 12713984 | tf_op jit(solution)/shard_map/sbcd,dbh->sbch/dot_general | solution.py:32
  325.5 0.0 copy-start.4
  325.5 1.4 collective-permute-start
  326.9 26.6 %collective-permute-done = f32[64,4,9,128]{3,0,2,1:T(8,128)S(1)} collective-permute-done((f32[64,4,9,128]{3,0,2,1:T(8,128)S(1)}, f32[64,4,9,128]{3,0,2,1:T(8,128)S(1)}, u32[]{:S(2)}, u32[]{:S(2)}) %collective-permute-start) | collective-permute-done | bytes 1179680 | tf_op jit(solution)/shard_map/ppermute | solution.py:41
  353.6 0.2 add.58
  353.7 3.0 collective-permute-start.1
  356.7 25.7 %collective-permute-done.1 = f32[64,4,9,128]{3,0,2,1:T(8,128)S(1)} collective-permute-done((f32[64,4,9,128]{3,0,2,1:T(8,128)S(1)}, f32[64,4,9,128]{3,0,2,1:T(8,128)S(1)}, u32[]{:S(2)}, u32[]{:S(2)}) %collective-permute-start.1) | collective-permute-done | bytes 1179680 | tf_op jit(solution)/shard_map/ppermute | solution.py:41
  382.4 0.0 copy-done
  382.4 0.0 copy-done.4
  382.4 2.8 convert_bitcast_fusion
  385.2 7.3 %copy.39 = bf16[64,4,9,2048]{3,1,2,0:T(4,128)(2,1)} copy(bf16[64,4,9,2048]{3,0,2,1:T(8,128)(2,1)S(1)} %convert_bitcast_fusion) | data formatting | bytes 18874368 | tf_op jit(solution)/shard_map/convert_element_type | solution.py:45
  392.5 6.5 all-to-all-start.1
  399.1 208.2 %all-to-all-done.1 = bf16[64,4,9,2048]{3,1,2,0:T(4,128)(2,1)} async-done(((bf16[64,4,9,2048]{3,1,2,0:T(4,128)(2,1)}), bf16[64,4,9,2048]{3,1,2,0:T(4,128)(2,1)}, u32[]{:S(2)}, u32[]{:S(2)}) %all-to-all-start.1) | async-done | bytes 9437216 | tf_op jit(solution)/shard_map/all_to_all | solution.py:44
  607.3 10.7 %copy.40 = bf16[64,4,9,2048]{3,2,1,0:T(8,128)(2,1)} copy(bf16[64,4,9,2048]{3,1,2,0:T(4,128)(2,1)} %all-to-all-done.1) | data formatting | bytes 18874368 | tf_op jit(solution)/shard_map/all_to_all | solution.py:44
  618.0 15.8 %reshape.75 = bf16[2304,2048]{1,0:T(8,128)(2,1)} reshape(bf16[64,4,9,2048]{3,2,1,0:T(8,128)(2,1)} %copy.40) | data formatting | bytes 18874368 | tf_op jit(solution)/shard_map/reshape | solution.py:53
  633.8 17.6 %gather_fusion.1 = bf16[1536,2048]{1,0:T(8,128)(2,1)} fusion(bf16[2304,2048]{1,0:T(8,128)(2,1)} %reshape.75, s32[2048]{0:T(1024)S(1)} %pad_clamp_fusion.1), kind=kCustom, calls=%fused_computation.1 | custom fusion | bytes 12589056 | tf_op jit(solution)/shard_map/gather | solution.py:54
  651.4 11.9 %reshape.76 = f32[384,4,2048]{2,1,0:T(4,128)} reshape(bf16[1536,2048]{1,0:T(8,128)(2,1)} %gather_fusion.1) | data formatting | bytes 18874368 | tf_op jit(solution)/shard_map/convert_element_type | solution.py:54
  663.3 0.0 copy-start.1
  663.3 11.9 %reduce_sum.32 = f32[384,2048]{1,0:T(8,128)} reduce(f32[384,4,2048]{2,1,0:T(4,128)} %reshape.76, f32[]{:T(128)} %constant.42.clone.1), dimensions={1}, to_apply=%region_6.7 | reduce | flops 2359296 | bytes 15728644 | tf_op jit(solution)/shard_map/reduce_sum | solution.py:55
  675.2 3.4 add_convert_fusion
  678.5 0.0 copy-done.1
  (9 shorter events, 0.1 us)
Async XLA Ops:
  0.0 382.4 %copy-start = (bf16[512,2048]{1,0:T(8,128)(2,1)S(1)}, bf16[512,2048]{1,0:T(8,128)(2,1)}, u32[]{:S(2)}) copy-start(bf16[512,2048]{1,0:T(8,128)(2,1)} %param.12) | copy-start | bytes 6291460
  2.3 1.4 copy-start.2
  5.5 10.7 %copy-start.3 = (f32[2048]{0:T(1024)S(1)}, f32[2048]{0:T(1024)}, u32[]{:S(2)}) copy-start(f32[2048]{0:T(1024)} %param.13) | copy-start | bytes 24580
  93.5 221.4 %all-to-all-start = ((bf16[64,4,9,2048]{3,1,2,0:T(4,128)(2,1)}), bf16[64,4,9,2048]{3,1,2,0:T(4,128)(2,1)}, u32[]{:S(2)}, u32[]{:S(2)}) async-start(bf16[64,4,9,2048]{3,1,2,0:T(4,128)(2,1)} %copy.36), calls=%async_computation | async-start | bytes 18874368 | tf_op jit(solution)/shard_map/all_to_all | solution.py:34
  325.5 56.8 %copy-start.4 = (f32[512]{0:T(512)S(1)}, f32[512]{0:T(512)}, u32[]{:S(2)}) copy-start(f32[512]{0:T(512)} %param.11) | copy-start | bytes 6148
  325.5 28.0 %collective-permute-start = (f32[64,4,9,128]{3,0,2,1:T(8,128)S(1)}, f32[64,4,9,128]{3,0,2,1:T(8,128)S(1)}, u32[]{:S(2)}, u32[]{:S(2)}) collective-permute-start(f32[64,4,9,128]{3,0,2,1:T(8,128)S(1)} %fusion.6), channel_id=1, source_target_pairs={{0,2},{2,0},{4,6},{6,4},{1,3},{3,1},{5,7},{7,5},{8,10},{10,8},{12,... | collective-permute-start | bytes 3538952 | tf_op jit(solution)/shard_map/ppermute | solution.py:41
  353.7 28.7 %collective-permute-start.1 = (f32[64,4,9,128]{3,0,2,1:T(8,128)S(1)}, f32[64,4,9,128]{3,0,2,1:T(8,128)S(1)}, u32[]{:S(2)}, u32[]{:S(2)}) collective-permute-start(f32[64,4,9,128]{3,0,2,1:T(8,128)S(1)} %add.58), channel_id=1, source_target_pairs={{0,4},{2,6},{4,0},{6,2},{1,5},{3,7},{5,1},{7,3},{8,12},{10,14},{12... | collective-permute-start | bytes 3538952 | tf_op jit(solution)/shard_map/ppermute | solution.py:41
  392.5 214.8 %all-to-all-start.1 = ((bf16[64,4,9,2048]{3,1,2,0:T(4,128)(2,1)}), bf16[64,4,9,2048]{3,1,2,0:T(4,128)(2,1)}, u32[]{:S(2)}, u32[]{:S(2)}) async-start(bf16[64,4,9,2048]{3,1,2,0:T(4,128)(2,1)} %copy.39), calls=%async_computation.1 | async-start | bytes 18874368 | tf_op jit(solution)/shard_map/all_to_all | solution.py:44
  663.3 15.3 %copy-start.1 = (bf16[512,2048]{1,0:T(8,128)(2,1)S(1)}, bf16[512,2048]{1,0:T(8,128)(2,1)}, u32[]{:S(2)}) copy-start(bf16[512,2048]{1,0:T(8,128)(2,1)} %param.12) | copy-start | bytes 6291460
